TPU v7x, 256 devices: a whole 4x4x8 slice. The times are simulated.
256 devices in a mesh: fsdp: 32 (over y, x, core), rep: 8 (over z).
Axes of the slice: x: 4, y: 4, z: 8, core: 2. Of those that a mesh axis runs over, the one named last changes fastest.
Arguments:
- tokens: bfloat16 [8, 4096, 2048], P('rep', 'fsdp'), may hold values from -6 to 6
- upstream: bfloat16 [8, 7168, 4096], P('rep', 'fsdp'), may hold values from -0.25 to 0.25
- weight: bfloat16 [2, 7168, 2048], P(None, 'fsdp'), may hold values from -0.125 to 0.125
- feedback: float32 [8, 2, 7168, 2048], P('rep', None, 'fsdp'), may hold values from -6 to 6
- momentum: float32 [2, 7168, 2048], P(None, 'fsdp', 'rep'), may hold values from -6 to 6
- right_factor: float32 [2, 7168, 64], P(None, 'fsdp'), may hold values from -6 to 6
Outputs:
- feedback_next: float32 [8, 2, 7168, 2048], P('rep', None, 'fsdp')
- momentum_next: float32 [2, 7168, 2048], P(None, 'fsdp', 'rep')
- weight_next: bfloat16 [2, 7168, 2048], P(None, 'fsdp', 'rep')
- right_next: float32 [2, 7168, 64], P(None, 'fsdp')
All inputs are finite; a program needn't handle non-finite values.
Results may differ from a plain program's by a relative error of at most 0.0023.
Values may be sent and summed in bfloat16 or wider, within the bound.
A program may use at most 128 MiB of HBM per device.

v0:
```python
import jax
import jax.numpy as jnp
from jax import lax
from jax.sharding import PartitionSpec as P

momentum_decay = 0.9
step_rate = 0.05
highest = lax.Precision.HIGHEST


def silu_pair(gate_pre):
    sigmoid = jax.nn.sigmoid(gate_pre)
    return (gate_pre * sigmoid, sigmoid * (1.0 + gate_pre * (1.0 - sigmoid)))


def solve_basis(factor, gram_matrix):
    lower_factor = jnp.linalg.cholesky(gram_matrix)
    return lax.linalg.triangular_solve(
        lower_factor, factor, left_side=False, lower=True, transpose_a=True
    )


def local_gram(factor):
    return jnp.einsum("kdr,kds->krs", factor, factor, precision=highest)


def per_device(tokens, upstream, weight, feedback, momentum, right_factor):
    own_rows = tokens[0]
    cotangents = upstream[0]
    contract_last = (((1,), (1,)), ((), ()))
    segment = lax.all_gather(own_rows, "fsdp", axis=0, tiled=True)
    cotangent_wide = cotangents.astype(jnp.float32)
    gate_pre = lax.dot_general(
        weight[0], segment, contract_last, preferred_element_type=jnp.float32
    )
    up_pre = lax.dot_general(weight[1], segment, contract_last, preferred_element_type=jnp.float32)
    activated, derivative = silu_pair(gate_pre)
    grad_gate = (cotangent_wide * up_pre * derivative).astype(jnp.bfloat16)
    grad_up = (cotangent_wide * activated).astype(jnp.bfloat16)
    term_gate = jnp.dot(grad_gate, segment, preferred_element_type=jnp.float32)
    term_up = jnp.dot(grad_up, segment, preferred_element_type=jnp.float32)
    gradient = jnp.stack([term_gate, term_up])
    delta = gradient + feedback[0]
    left_part = jnp.einsum("kfd,kfr->kdr", delta, right_factor, precision=highest)
    replicas = lax.axis_size("rep")
    left_mean = lax.psum(left_part, ("fsdp", "rep")) / replicas
    basis = solve_basis(left_mean, local_gram(left_mean))
    right_part = jnp.einsum("kfd,kdr->kfr", delta, basis, precision=highest)
    right_next = lax.psum(right_part, "rep") / replicas
    approx = jnp.einsum("kdr,kfr->kfd", basis, right_next, precision=highest)
    feedback_next = (delta - approx)[None]
    slab_cols = momentum.shape[2]
    slab_start = lax.axis_index("rep") * slab_cols
    approx_slab = lax.dynamic_slice_in_dim(approx, slab_start, slab_cols, 2)
    weight_slab = lax.dynamic_slice_in_dim(weight, slab_start, slab_cols, 2)
    momentum_next = momentum_decay * momentum + approx_slab
    weight_next = (weight_slab.astype(jnp.float32) - step_rate * momentum_next).astype(jnp.bfloat16)
    return (feedback_next, momentum_next, weight_next, right_next)


def solution(mesh):
    placed = (
        P("rep", "fsdp", None),
        P("rep", "fsdp", None),
        P(None, "fsdp", None),
        P("rep", None, "fsdp", None),
        P(None, "fsdp", "rep"),
        P(None, "fsdp", None),
    )
    return jax.shard_map(
        per_device,
        mesh=mesh,
        in_specs=placed,
        out_specs=(
            P("rep", None, "fsdp", None),
            P(None, "fsdp", "rep"),
            P(None, "fsdp", "rep"),
            P(None, "fsdp", None),
        ),
        check_vma=False,
    )
```

profile of v0, /device:TPU:2, one launch (start us, length us, event | category | flops | bytes accessed | tf_op | source)
XLA Modules:
  0.0 520.9 jit_solution(15495969798062645339)
XLA Ops:
  7.2 0.0 copy-start
  7.2 0.0 all-gather.3.cloned.1.call-start
  7.2 0.7 all-gather.3.cloned.1.call-update
  7.9 0.0 all-reduce.3.cloned.1.call-start
  8.0 83.1 %all-gather.3.cloned.1.call-done = bf16[1,4096,2048]{2,1,0:T(8,128)(2,1)} async-done(((bf16[1,128,2048]{2,1,0:T(8,128)(2,1)}), bf16[1,4096,2048]{2,1,0:T(8,128)(2,1)}) %all-gather.3.cloned.1.call-update) | async-done | bytes 16777232 | tf_op jit(solution)/shard_map/all_gather | solution.py:31
  91.1 13.0 %fusion.4 = f32[224,4096]{1,0:T(8,128)} fusion(bf16[1,4096,2048]{2,1,0:T(8,128)(2,1)} %all-gather.3.cloned.1.call-done, bf16[2,224,2048]{2,1,0:T(8,128)(2,1)} %param.8), kind=kOutput, calls=%fused_computation.4 | convolution fusion | flops 3758096384 | bytes 21364736 | tf_op jit(solution)/shard_map/dot_general | solution.py:33
  104.1 20.5 %fusion.25 = f32[1,224,2048]{2,1,0:T(8,128)S(1)} fusion(bf16[1,4096,2048]{2,1,0:T(8,128)(2,1)} %all-gather.3.cloned.1.call-done, f32[224,4096]{1,0:T(8,128)} %fusion.4, bf16[1,224,4096]{2,1,0:T(8,128)(2,1)} %param.7, bf16[2,224,2048]{2,1,0:T(8,128)(2,1)} %param.8), kind=kOutput, calls=%fused_computation.21 | convolution fusion | flops 7526285312 | bytes 41811968 | tf_op jit(solution)/shard_map/dot_general | solution.py:40
  124.7 0.0 copy-start.1
  124.7 9.7 %fusion.30 = f32[1,224,2048]{2,1,0:T(8,128)S(1)} fusion(bf16[1,4096,2048]{2,1,0:T(8,128)(2,1)} %all-gather.3.cloned.1.call-done, f32[224,4096]{1,0:T(8,128)} %fusion.4, bf16[1,224,4096]{2,1,0:T(8,128)(2,1)} %param.7), kind=kOutput, calls=%fused_computation.22 | convolution fusion | flops 3764518912 | bytes 24117248 | tf_op jit(solution)/shard_map/dot_general | solution.py:41
  134.4 0.0 copy-start.3
  134.4 1.2 copy-done.3
  135.7 3.6 fusion.57
  139.3 0.0 all-reduce.3.cloned.1.call-update
  139.3 0.2 all-reduce.5.cloned.1.call-start
  139.6 258.4 %all-reduce.3.cloned.1.call-done = f32[2,2048,64]{1,2,0:T(8,128)} async-done(((f32[2,2048,64]{1,2,0:T(8,128)}), f32[2,2048,64]{1,2,0:T(8,128)}) %all-reduce.3.cloned.1.call-update) | async-done | bytes 1048592 | tf_op jit(solution)/shard_map/psum | solution.py:46
  397.9 2.7 fusion.40
  400.6 0.1 copy.12
  400.7 11.7 %custom-call.7 = f32[2,64,64]{2,1,0:T(8,128)S(1)} custom-call(f32[2,64,64]{2,1,0:T(8,128)S(1)} %fusion.51), custom_call_target="Cholesky" | custom-call | tf_op jit(solution)/shard_map/jit(cholesky)/cholesky | solution.py:17
  412.5 0.1 compare_reduce_fusion
  412.6 0.1 select_bitcast_fusion
  412.7 9.8 %custom-call.8 = f32[2,1,64,64]{2,3,1,0:T(8,128)S(1)} custom-call(f32[2,1,64,64]{3,2,1,0:T(8,128)S(1)} %select_bitcast_fusion), custom_call_target="InvertDiagBlocksLowerTriangular" | custom-call | tf_op jit(solution)/shard_map/triangular_solve | solution.py:18
  422.5 2.3 fusion.38
  424.9 7.1 %fusion.56 = f32[2,224,64]{1,2,0:T(8,128)} fusion(f32[2,2048,64]{1,2,0:T(8,128)S(1)} %fusion.38, f32[1,224,2048]{2,1,0:T(8,128)} %copy-done.3, f32[1,224,2048]{2,1,0:T(8,128)S(1)} %fusion.25, f32[1,2,224,2048]{3,2,1,0:T(8,128)} %param.9), kind=kOutput, calls=%fused_computation.52 | convolution fusion | flops 706478080 | bytes 8503296 | tf_op jit(solution)/shard_map/kfd,kdr->kfr/dot_general | solution.py:48
  432.0 0.0 all-reduce.5.cloned.1.call-update
  432.0 71.5 %all-reduce.5.cloned.1.call-done = f32[2,224,64]{1,2,0:T(8,128)} async-done(((f32[2,224,64]{1,2,0:T(8,128)}), f32[2,224,64]{1,2,0:T(8,128)}) %all-reduce.5.cloned.1.call-update) | async-done | bytes 114704 | tf_op jit(solution)/shard_map/psum | solution.py:49
  503.5 1.1 broadcast_multiply_fusion
  504.5 0.0 copy-start.4
  504.5 3.1 fusion.58
  507.6 0.0 copy-start.5
  507.6 4.8 subtract_bitcast_fusion
  512.5 0.0 copy-done.5
  512.5 1.9 subtract_convert_fusion
  (9 shorter events, 0.1 us)
Async XLA Ops:
  7.2 128.5 %copy-start = (f32[2,224,64]{1,2,0:T(8,128)S(1)}, f32[2,224,64]{1,2,0:T(8,128)}, u32[]{:S(2)}) copy-start(f32[2,224,64]{1,2,0:T(8,128)} %param.11) | copy-start | bytes 344068
  7.2 83.9 %all-gather.3.cloned.1.call-start = ((), (), s32[]{:S(2)}) async-start(), calls=%async_computation.2 | async-start | bytes 17301504 | tf_op jit(solution)/shard_map/all_gather | solution.py:31
  7.9 390.0 %all-reduce.3.cloned.1.call-start = ((), (), s32[]{:S(2)}) async-start(), calls=%async_computation | async-start | bytes 2097152 | tf_op jit(solution)/shard_map/psum | solution.py:46
  124.7 11.0 %copy-start.1 = (f32[1,2,224,2048]{3,2,1,0:T(8,128)S(1)}, f32[1,2,224,2048]{3,2,1,0:T(8,128)}, u32[]{:S(2)}) copy-start(f32[1,2,224,2048]{3,2,1,0:T(8,128)} %param.9) | copy-start | bytes 11010052
  134.4 1.3 copy-start.3
  139.3 364.2 %all-reduce.5.cloned.1.call-start = ((), (), s32[]{:S(2)}) async-start(), calls=%async_computation.1 | async-start | bytes 262144 | tf_op jit(solution)/shard_map/psum | solution.py:49
  503.5 4.2 copy-start.2
  504.5 8.0 %copy-start.4 = (f32[2,224,64]{1,2,0:T(8,128)}, f32[2,224,64]{1,2,0:T(8,128)S(1)}, u32[]{:S(2)}) copy-start(f32[2,224,64]{1,2,0:T(8,128)S(1)} %broadcast_multiply_fusion) | copy-start | bytes 344068
  507.6 4.9 copy-start.5
Sparse Core Ops, SparseCore 0:
  10.5 80.4 all-gather.2
  139.4 258.4 all-reduce.2
  432.1 71.3 all-reduce.4
where the time goes:
time: 521 us
  waiting for transfers between devices  414 us (79%)
  matrix products  62.1 us (12%)
  other arithmetic  29.6 us (6%)
  between operations  13.9 us (3%)
    psum x1, waiting for transfers between devices, per_device(): left_mean = lax.psum(left_part, ('fsdp', 'rep')) / replicas  258 us
    all_gather x1, waiting for transfers between devices, per_device(): segment = lax.all_gather(own_rows, 'fsdp', axis=0, tiled=True)  83.1 us
    psum x1, waiting for transfers between devices, per_device(): right_next = lax.psum(right_part, 'rep') / replicas  71.5 us
    dot_general x1, matrix products, per_device(): term_gate = jnp.dot(grad_gate, segment, preferred_element_type=jnp.float32)  20.5 us
    dot_general x1, matrix products, per_device(): lax.dot_general(weight[0], segment, contract_last, preferred_element_type...  13 us
    another operation x4, other arithmetic, solve_basis(): lower_factor = jnp.linalg.cholesky(gram_matrix)  11.9 us
  transfers between devices with their start and end apart: 3, of which 3 were waited for; matrix products, arithmetic and copies ran while one was open for 0% of the time, Pallas kernels for 0%

commit v1 on v0

--- a/solution.py
+++ b/solution.py
@@ -28,7 +28,9 @@
     own_rows = tokens[0]
     cotangents = upstream[0]
     contract_last = (((1,), (1,)), ((), ()))
-    segment = lax.all_gather(own_rows, "fsdp", axis=0, tiled=True)
+    segment = jnp.concatenate(
+        lax.all_to_all(jnp.stack([own_rows] * lax.axis_size("fsdp"), axis=0), "fsdp", 0, 0), axis=0
+    )
     cotangent_wide = cotangents.astype(jnp.float32)
     gate_pre = lax.dot_general(
         weight[0], segment, contract_last, preferred_element_type=jnp.float32

time: 521 us -> 631 us (1.21)
  blocking collectives: 0 us -> 192 us
  waiting for transfers between devices: 414 us -> 331 us
    all_to_all x0 -> x1, blocking collectives: none -> 192 us  [per_device(): lax.all_to_all(jnp.stack([own_rows] * lax.axis_size('fsdp'), axis=0), 'fs...]
    all_gather x1 -> x0, waiting for transfers between devices: 83.1 us -> none  [per_device(): segment = lax.all_gather(own_rows, 'fsdp', axis=0, tiled=True)]
  transfers between devices with their start and end apart: 3 -> 2, of which waited for: 3 -> 2; matrix products, arithmetic and copies ran while one was open for 0% -> 0% of each run, Pallas kernels for 0% -> 0%
where the time goes in v1:
time: 631 us
  waiting for transfers between devices  331 us (52%)
  blocking collectives  192 us (30%)
  matrix products  59.2 us (9%)
  other arithmetic  29.6 us (5%)
  between operations  14.2 us (2%)
    psum x1, waiting for transfers between devices, per_device(): left_mean = lax.psum(left_part, ('fsdp', 'rep')) / replicas  259 us
    all_to_all x1, blocking collectives, per_device(): lax.all_to_all(jnp.stack([own_rows] * lax.axis_size('fsdp'), axis=0), 'fs...  192 us
    psum x1, waiting for transfers between devices, per_device(): right_next = lax.psum(right_part, 'rep') / replicas  71.5 us
    dot_general x1, matrix products, per_device(): term_gate = jnp.dot(grad_gate, segment, preferred_element_type=jnp.float32)  20.2 us
  transfers between devices with their start and end apart: 2, of which 2 were waited for; matrix products, arithmetic and copies ran while one was open for 0% of the time, Pallas kernels for 0%

profile of v1, /device:TPU:2, one launch (start us, length us, event | category | flops | bytes accessed | tf_op | source)
XLA Modules:
  0.0 631.0 jit_solution(16134316759440331017)
XLA Ops:
  7.2 0.0 copy-start
  7.2 0.0 all-reduce.3.cloned.1.call-start
  7.2 3.6 stack.12
  10.8 0.0 copy-start.6
  10.9 192.2 %all_to_all.5 = bf16[32,128,2048]{2,1,0:T(8,128)(2,1)} all-to-all(bf16[32,128,2048]{2,1,0:T(8,128)(2,1)S(1)} %stack.12), channel_id=1, replica_groups=mesh['fsdp'=32,'rep'=8] {'fsdp'}, dimensions={0} | all-to-all | bytes 33554432 | tf_op jit(solution)/shard_map/all_to_all | solution.py:32
  203.0 10.6 %fusion.10 = f32[224,4096]{1,0:T(8,128)} fusion(bf16[4096,2048]{1,0:T(8,128)(2,1)} %bitcast.48, bf16[2,224,2048]{2,1,0:T(8,128)(2,1)S(1)} %copy-done.6), kind=kOutput, calls=%fused_computation.16 | convolution fusion | flops 3758096384 | bytes 21364736 | tf_op jit(solution)/shard_map/dot_general | solution.py:35
  213.6 20.2 %convolution_bitcast_fusion.1 = f32[1,224,2048]{2,1,0:T(8,128)S(1)} fusion(bf16[4096,2048]{1,0:T(8,128)(2,1)} %bitcast.49, f32[224,4096]{1,0:T(8,128)} %fusion.10, bf16[1,224,4096]{2,1,0:T(8,128)(2,1)} %param.7, bf16[2,224,2048]{2,1,0:T(8,128)(2,1)} %param.8), kind=kOutput, calls=%fused_computation.9 | convolution fusion | flops 7526285312 | bytes 41811968 | tf_op jit(solution)/shard_map/dot_general | solution.py:42
  233.8 0.0 copy-start.1
  233.8 9.7 %convolution_bitcast_fusion = f32[1,224,2048]{2,1,0:T(8,128)S(1)} fusion(bf16[4096,2048]{1,0:T(8,128)(2,1)} %bitcast.50, f32[224,4096]{1,0:T(8,128)} %fusion.10, bf16[1,224,4096]{2,1,0:T(8,128)(2,1)} %param.7), kind=kOutput, calls=%fused_computation.8 | convolution fusion | flops 3764518912 | bytes 24117248 | tf_op jit(solution)/shard_map/dot_general | solution.py:43
  243.5 1.2 copy-done.3
  244.8 0.0 copy-done
  244.8 3.6 fusion.26
  248.4 0.0 all-reduce.3.cloned.1.call-update
  248.4 0.2 all-reduce.5.cloned.1.call-start
  248.7 259.0 %all-reduce.3.cloned.1.call-done = f32[2,2048,64]{1,2,0:T(8,128)} async-done(((f32[2,2048,64]{1,2,0:T(8,128)}), f32[2,2048,64]{1,2,0:T(8,128)}) %all-reduce.3.cloned.1.call-update) | async-done | bytes 1048592 | tf_op jit(solution)/shard_map/psum | solution.py:48
  507.7 2.7 fusion.8
  510.4 0.1 copy.12
  510.5 11.7 %custom-call.7 = f32[2,64,64]{2,1,0:T(8,128)S(1)} custom-call(f32[2,64,64]{2,1,0:T(8,128)S(1)} %fusion.20), custom_call_target="Cholesky" | custom-call | tf_op jit(solution)/shard_map/jit(cholesky)/cholesky | solution.py:17
  522.3 0.1 compare_reduce_fusion
  522.4 0.1 select_bitcast_fusion
  522.5 9.8 %custom-call.8 = f32[2,1,64,64]{2,3,1,0:T(8,128)S(1)} custom-call(f32[2,1,64,64]{3,2,1,0:T(8,128)S(1)} %select_bitcast_fusion), custom_call_target="InvertDiagBlocksLowerTriangular" | custom-call | tf_op jit(solution)/shard_map/triangular_solve | solution.py:18
  532.3 2.3 fusion.6
  534.6 7.1 %fusion.25 = f32[2,224,64]{1,2,0:T(8,128)} fusion(f32[2,2048,64]{1,2,0:T(8,128)S(1)} %fusion.6, f32[1,224,2048]{2,1,0:T(8,128)} %copy-done.3, f32[1,224,2048]{2,1,0:T(8,128)S(1)} %convolution_bitcast_fusion.1, f32[1,2,224,2048]{3,2,1,0:T(8,128)} %param.9), kind=kOutput, calls=%fused_computation.38 | convolution fusion | flops 706478080 | bytes 8503296 | tf_op jit(solution)/shard_map/kfd,kdr->kfr/dot_general | solution.py:50
  541.7 0.0 all-reduce.5.cloned.1.call-update
  541.8 71.5 %all-reduce.5.cloned.1.call-done = f32[2,224,64]{1,2,0:T(8,128)} async-done(((f32[2,224,64]{1,2,0:T(8,128)}), f32[2,224,64]{1,2,0:T(8,128)}) %all-reduce.5.cloned.1.call-update) | async-done | bytes 114704 | tf_op jit(solution)/shard_map/psum | solution.py:51
  613.2 1.1 broadcast_multiply_fusion
  614.3 0.0 copy-start.4
  614.3 3.1 fusion.27
  617.4 0.0 copy-start.5
  617.4 4.8 subtract_bitcast_fusion
  622.2 0.0 copy-done.5
  622.2 1.9 subtract_convert_fusion
  (10 shorter events, 0.1 us)
Async XLA Ops:
  7.2 237.6 %copy-start = (f32[2,224,64]{1,2,0:T(8,128)S(1)}, f32[2,224,64]{1,2,0:T(8,128)}, u32[]{:S(2)}) copy-start(f32[2,224,64]{1,2,0:T(8,128)} %param.11) | copy-start | bytes 344068
  7.2 500.5 %all-reduce.3.cloned.1.call-start = ((), (), s32[]{:S(2)}) async-start(), calls=%async_computation.1 | async-start | bytes 2097152 | tf_op jit(solution)/shard_map/psum | solution.py:48
  10.8 192.2 %copy-start.6 = (bf16[2,224,2048]{2,1,0:T(8,128)(2,1)S(1)}, bf16[2,224,2048]{2,1,0:T(8,128)(2,1)}, u32[]{:S(2)}) copy-start(bf16[2,224,2048]{2,1,0:T(8,128)(2,1)} %param.8) | copy-start | bytes 5505028
  233.8 11.0 %copy-start.1 = (f32[1,2,224,2048]{3,2,1,0:T(8,128)S(1)}, f32[1,2,224,2048]{3,2,1,0:T(8,128)}, u32[]{:S(2)}) copy-start(f32[1,2,224,2048]{3,2,1,0:T(8,128)} %param.9) | copy-start | bytes 11010052
  243.5 1.3 copy-start.3
  248.4 364.8 %all-reduce.5.cloned.1.call-start = ((), (), s32[]{:S(2)}) async-start(), calls=%async_computation.2 | async-start | bytes 262144 | tf_op jit(solution)/shard_map/psum | solution.py:51
  613.2 4.2 copy-start.2
  614.3 8.0 %copy-start.4 = (f32[2,224,64]{1,2,0:T(8,128)}, f32[2,224,64]{1,2,0:T(8,128)S(1)}, u32[]{:S(2)}) copy-start(f32[2,224,64]{1,2,0:T(8,128)S(1)} %broadcast_multiply_fusion) | copy-start | bytes 344068
  617.4 4.9 copy-start.5
Sparse Core Ops, SparseCore 0:
  248.5 259.1 all-reduce.2
  541.9 71.3 all-reduce.4

commit v2 on v0

--- a/solution.py
+++ b/solution.py
@@ -6,6 +6,11 @@
 momentum_decay = 0.9
 step_rate = 0.05
 highest = lax.Precision.HIGHEST
+
+
+def quarters_draw(matrix):
+    piece_next = jax.lax.psum(jax.lax.psum(matrix, "rep"), "fsdp")
+    return piece_next
 
 
 def silu_pair(gate_pre):
@@ -43,7 +48,7 @@
     delta = gradient + feedback[0]
     left_part = jnp.einsum("kfd,kfr->kdr", delta, right_factor, precision=highest)
     replicas = lax.axis_size("rep")
-    left_mean = lax.psum(left_part, ("fsdp", "rep")) / replicas
+    left_mean = quarters_draw(left_part) / replicas
     basis = solve_basis(left_mean, local_gram(left_mean))
     right_part = jnp.einsum("kfd,kdr->kfr", delta, basis, precision=highest)
     right_next = lax.psum(right_part, "rep") / replicas

time: 521 us -> 456 us (0.88)
  waiting for transfers between devices: 414 us -> 349 us
    psum x1 -> x2, waiting for transfers between devices: 258 us -> 192 us  [quarters_draw(): piece_next = jax.lax.psum(jax.lax.psum(matrix, 'rep'), 'fsdp')]
  transfers between devices with their start and end apart: 3 -> 4, of which waited for: 3 -> 4; matrix products, arithmetic and copies ran while one was open for 0% -> 0% of each run, Pallas kernels for 0% -> 0%
where the time goes in v2:
time: 456 us
  waiting for transfers between devices  349 us (77%)
  matrix products  62.1 us (14%)
  other arithmetic  29.6 us (6%)
  between operations  13.9 us (3%)
    psum x2, waiting for transfers between devices, quarters_draw(): piece_next = jax.lax.psum(jax.lax.psum(matrix, 'rep'), 'fsdp')  192 us
    all_gather x1, waiting for transfers between devices, per_device(): segment = lax.all_gather(own_rows, 'fsdp', axis=0, tiled=True)  83.1 us
    psum x1, waiting for transfers between devices, per_device(): right_next = lax.psum(right_part, 'rep') / replicas  73 us
    dot_general x1, matrix products, per_device(): term_gate = jnp.dot(grad_gate, segment, preferred_element_type=jnp.float32)  20.5 us
    dot_general x1, matrix products, per_device(): lax.dot_general(weight[0], segment, contract_last, preferred_element_type...  13 us
    another operation x4, other arithmetic, solve_basis(): lower_factor = jnp.linalg.cholesky(gram_matrix)  11.9 us
    another operation x3, other arithmetic, solve_basis(): lax.linalg.triangular_solve(lower_factor, factor, left_side=False, lower=...  9.92 us
    dot_general x1, matrix products, per_device(): term_up = jnp.dot(grad_up, segment, preferred_element_type=jnp.float32)  9.73 us
  transfers between devices with their start and end apart: 4, of which 4 were waited for; matrix products, arithmetic and copies ran while one was open for 0% of the time, Pallas kernels for 0%

profile of v2, /device:TPU:2, one launch (start us, length us, event | category | flops | bytes accessed | tf_op | source)
XLA Modules:
  0.0 456.1 jit_solution(18000397189045079013)
XLA Ops:
  7.2 0.0 copy-start
  7.2 0.0 all-gather.3.cloned.1.call-start
  7.2 0.7 all-gather.3.cloned.1.call-update
  7.9 0.0 all-reduce.4.cloned.1.call-start
  8.0 83.1 %all-gather.3.cloned.1.call-done = bf16[1,4096,2048]{2,1,0:T(8,128)(2,1)} async-done(((bf16[1,128,2048]{2,1,0:T(8,128)(2,1)}), bf16[1,4096,2048]{2,1,0:T(8,128)(2,1)}) %all-gather.3.cloned.1.call-update) | async-done | bytes 16777232 | tf_op jit(solution)/shard_map/all_gather | solution.py:36
  91.1 13.0 %fusion.4 = f32[224,4096]{1,0:T(8,128)} fusion(bf16[1,4096,2048]{2,1,0:T(8,128)(2,1)} %all-gather.3.cloned.1.call-done, bf16[2,224,2048]{2,1,0:T(8,128)(2,1)} %param.8), kind=kOutput, calls=%fused_computation.4 | convolution fusion | flops 3758096384 | bytes 21364736 | tf_op jit(solution)/shard_map/dot_general | solution.py:38
  104.1 20.5 %fusion.25 = f32[1,224,2048]{2,1,0:T(8,128)S(1)} fusion(bf16[1,4096,2048]{2,1,0:T(8,128)(2,1)} %all-gather.3.cloned.1.call-done, f32[224,4096]{1,0:T(8,128)} %fusion.4, bf16[1,224,4096]{2,1,0:T(8,128)(2,1)} %param.7, bf16[2,224,2048]{2,1,0:T(8,128)(2,1)} %param.8), kind=kOutput, calls=%fused_computation.21 | convolution fusion | flops 7526285312 | bytes 41811968 | tf_op jit(solution)/shard_map/dot_general | solution.py:45
  124.7 9.7 %fusion.30 = f32[1,224,2048]{2,1,0:T(8,128)S(1)} fusion(bf16[1,4096,2048]{2,1,0:T(8,128)(2,1)} %all-gather.3.cloned.1.call-done, f32[224,4096]{1,0:T(8,128)} %fusion.4, bf16[1,224,4096]{2,1,0:T(8,128)(2,1)} %param.7), kind=kOutput, calls=%fused_computation.22 | convolution fusion | flops 3764518912 | bytes 24117248 | tf_op jit(solution)/shard_map/dot_general | solution.py:46
  134.4 1.2 copy-done.3
  135.7 3.6 fusion.57
  139.3 0.0 all-reduce.4.cloned.1.call-update
  139.3 0.0 all-reduce.6.cloned.1.call-start
  139.3 75.7 %all-reduce.4.cloned.1.call-done = f32[2,2048,64]{1,2,0:T(8,128)} async-done(((f32[2,2048,64]{1,2,0:T(8,128)}), f32[2,2048,64]{1,2,0:T(8,128)}) %all-reduce.4.cloned.1.call-update) | async-done | bytes 1048592 | tf_op jit(solution)/shard_map/psum | solution.py:12
  215.0 0.0 all-reduce.6.cloned.1.call-update
  215.0 0.2 all-reduce.8.cloned.1.call-start
  215.3 116.2 %all-reduce.6.cloned.1.call-done = f32[2,2048,64]{1,2,0:T(8,128)} async-done(((f32[2,2048,64]{1,2,0:T(8,128)}), f32[2,2048,64]{1,2,0:T(8,128)}) %all-reduce.6.cloned.1.call-update) | async-done | bytes 1048592 | tf_op jit(solution)/shard_map/psum | solution.py:12
  331.5 2.7 fusion.40
  334.2 0.1 copy.12
  334.3 11.7 %custom-call.7 = f32[2,64,64]{2,1,0:T(8,128)S(1)} custom-call(f32[2,64,64]{2,1,0:T(8,128)S(1)} %fusion.51), custom_call_target="Cholesky" | custom-call | tf_op jit(solution)/shard_map/jit(cholesky)/cholesky | solution.py:22
  346.1 0.1 compare_reduce_fusion
  346.2 0.1 select_bitcast_fusion
  346.3 9.8 %custom-call.8 = f32[2,1,64,64]{2,3,1,0:T(8,128)S(1)} custom-call(f32[2,1,64,64]{3,2,1,0:T(8,128)S(1)} %select_bitcast_fusion), custom_call_target="InvertDiagBlocksLowerTriangular" | custom-call | tf_op jit(solution)/shard_map/triangular_solve | solution.py:23
  356.1 2.3 fusion.38
  358.5 7.1 %fusion.56 = f32[2,224,64]{1,2,0:T(8,128)} fusion(f32[2,2048,64]{1,2,0:T(8,128)S(1)} %fusion.38, f32[1,224,2048]{2,1,0:T(8,128)} %copy-done.3, f32[1,224,2048]{2,1,0:T(8,128)S(1)} %fusion.25, f32[1,2,224,2048]{3,2,1,0:T(8,128)} %param.9), kind=kOutput, calls=%fused_computation.52 | convolution fusion | flops 706478080 | bytes 8503296 | tf_op jit(solution)/shard_map/kfd,kdr->kfr/dot_general | solution.py:53
  365.6 0.0 all-reduce.8.cloned.1.call-update
  365.6 73.0 %all-reduce.8.cloned.1.call-done = f32[2,224,64]{1,2,0:T(8,128)} async-done(((f32[2,224,64]{1,2,0:T(8,128)}), f32[2,224,64]{1,2,0:T(8,128)}) %all-reduce.8.cloned.1.call-update) | async-done | bytes 114704 | tf_op jit(solution)/shard_map/psum | solution.py:54
  438.6 1.1 broadcast_multiply_fusion
  439.7 0.0 copy-start.4
  439.7 3.1 fusion.58
  442.8 0.0 copy-start.5
  442.8 4.8 %subtract_bitcast_fusion = f32[1,2,224,2048]{3,2,1,0:T(8,128)} fusion(f32[2,224,2048]{2,1,0:T(8,128)S(1)} %fusion.58, f32[1,2,224,2048]{3,2,1,0:T(8,128)S(1)} %copy-done.2, f32[1,224,2048]{2,1,0:T(8,128)} %copy-done.3, f32[1,224,2048]{2,1,0:T(8,128)S(1)} %fusion.25), kind=kLoop, calls=%fused_computation.15 | loop fusion | flops 2752512 | bytes 14680064 | tf_op jit(solution)/shard_map/broadcast_in_dim | solution.py:56
  447.7 1.9 subtract_convert_fusion
  (12 shorter events, 0.1 us)
Async XLA Ops:
  7.2 128.5 %copy-start = (f32[2,224,64]{1,2,0:T(8,128)S(1)}, f32[2,224,64]{1,2,0:T(8,128)}, u32[]{:S(2)}) copy-start(f32[2,224,64]{1,2,0:T(8,128)} %param.11) | copy-start | bytes 344068
  7.2 83.9 %all-gather.3.cloned.1.call-start = ((), (), s32[]{:S(2)}) async-start(), calls=%async_computation.3 | async-start | bytes 17301504 | tf_op jit(solution)/shard_map/all_gather | solution.py:36
  7.9 207.1 %all-reduce.4.cloned.1.call-start = ((), (), s32[]{:S(2)}) async-start(), calls=%async_computation | async-start | bytes 2097152 | tf_op jit(solution)/shard_map/psum | solution.py:12
  124.7 11.0 %copy-start.1 = (f32[1,2,224,2048]{3,2,1,0:T(8,128)S(1)}, f32[1,2,224,2048]{3,2,1,0:T(8,128)}, u32[]{:S(2)}) copy-start(f32[1,2,224,2048]{3,2,1,0:T(8,128)} %param.9) | copy-start | bytes 11010052
  134.4 1.3 copy-start.3
  139.3 192.3 %all-reduce.6.cloned.1.call-start = ((), (), s32[]{:S(2)}) async-start(), calls=%async_computation.1 | async-start | bytes 2097152 | tf_op jit(solution)/shard_map/psum | solution.py:12
  215.0 223.6 %all-reduce.8.cloned.1.call-start = ((), (), s32[]{:S(2)}) async-start(), calls=%async_computation.2 | async-start | bytes 262144 | tf_op jit(solution)/shard_map/psum | solution.py:54
  438.6 4.2 copy-start.2
  439.7 8.0 %copy-start.4 = (f32[2,224,64]{1,2,0:T(8,128)}, f32[2,224,64]{1,2,0:T(8,128)S(1)}, u32[]{:S(2)}) copy-start(f32[2,224,64]{1,2,0:T(8,128)S(1)} %broadcast_multiply_fusion) | copy-start | bytes 344068
  442.8 4.9 %copy-start.5 = (f32[2,224,256]{2,1,0:T(8,128)S(1)}, f32[2,224,256]{2,1,0:T(8,128)}, u32[]{:S(2)}) copy-start(f32[2,224,256]{2,1,0:T(8,128)} %param.10) | copy-start | bytes 1376260
Sparse Core Ops, SparseCore 0:
  10.5 80.4 all-gather.2
  139.4 75.5 all-reduce.3
  218.2 113.2 all-reduce.5
  365.7 72.8 all-reduce.7
